TPU v7x, 32 devices: a whole 2x2x4 slice. The times are simulated.
32 devices in a mesh: gx: 16 (over z, y, core), gy: 2 (over x).
Axes of the slice: x: 2, y: 2, z: 4, core: 2. Of those that a mesh axis runs over, the one named last changes fastest.
Arguments:
- field: float32 [6, 16, 256, 256], P(None, None, 'gx', 'gy'), may hold values from -6 to 6
- driver: float32 [6, 16, 256, 256], P(None, None, 'gx', 'gy'), may hold values from -6 to 6
- east_wind: float32 [16, 256, 256], P(None, 'gx', 'gy'), may hold values from -0.4 to 0.4
- north_wind: float32 [16, 256, 256], P(None, 'gx', 'gy'), may hold values from -0.4 to 0.4
Outputs:
- advected: float32 [6, 16, 256, 256], P(None, None, 'gx', 'gy')
- coeffs: float32 [6, 16, 4096], replicated
All inputs are finite; a program needn't handle non-finite values.
Results may differ from a plain program's by a relative error of at most 0.000098.
Values sent between devices are 32-bit elements; how exact they have to be, the bound alone decides.
A program may use at most 128 MiB of HBM per device.

v0:
```python
import math
import jax
import jax.numpy as jnp
from jax import lax
from jax.sharding import PartitionSpec as P

MX = 64
MY = 64


def shifted(value, axis, steps):
    count = lax.axis_size(axis)
    first, last = (max(0, -steps), min(count, count - steps))
    return lax.ppermute(value, axis, [(source, source + steps) for source in range(first, last)])


def padded(x, sides, width):
    for axis, dim in sides:
        peers, length = (lax.axis_size(axis), x.shape[dim])
        up = [(i, (i + 1) % peers) for i in range(peers - 1)]
        down = [(j, i) for i, j in up]
        last = lax.slice_in_dim(x, length - width, length, axis=dim)
        first = lax.slice_in_dim(x, 0, width, axis=dim)
        before = lax.ppermute(last, axis, up)
        after = lax.ppermute(first, axis, down)
        x = jnp.concatenate([before, x, after], axis=dim)
    return x


def cosine_table(first, count, total, modes):
    indices = first + jnp.arange(count, dtype=jnp.int32)
    wavenum = jnp.arange(modes, dtype=jnp.int32)
    phases = (wavenum[None, :] * (2 * indices[:, None] + 1)).astype(jnp.float32)
    cosines = jnp.cos(phases * (math.pi / (2.0 * total)))
    weight = jnp.where(wavenum == 0, math.sqrt(1.0 / total), math.sqrt(2.0 / total)).astype(
        jnp.float32
    )
    return cosines * weight[None, :]


def upwind(tracer, winds):
    east = winds[0]
    north = winds[1]
    east_flux = (
        jnp.maximum(east[:, :-1, :], 0.0) * tracer[..., :-1, :]
        + jnp.minimum(east[:, :-1, :], 0.0) * tracer[..., 1:, :]
    )
    north_flux = (
        jnp.maximum(north[:, :, :-1], 0.0) * tracer[..., :, :-1]
        + jnp.minimum(north[:, :, :-1], 0.0) * tracer[..., :, 1:]
    )
    inner = tracer[..., 1:-1, 1:-1]
    inner = inner - (east_flux[..., 1:, 1:-1] - east_flux[..., :-1, 1:-1])
    return inner - (north_flux[..., 1:-1, 1:] - north_flux[..., 1:-1, :-1])


def shards(field, driver, east_wind, north_wind):
    high = lax.Precision.HIGHEST
    tracers, levels, strip_cols, band_rows = field.shape
    nx_total = strip_cols * lax.axis_size("gx")
    ny_total = band_rows * lax.axis_size("gy")
    x_first = lax.axis_index("gx") * strip_cols
    y_first = lax.axis_index("gy") * band_rows
    x_table = cosine_table(x_first, strip_cols, nx_total, MX)
    y_table = cosine_table(y_first, band_rows, ny_total, MY)
    departure = driver - field
    half_proj = jnp.einsum("tlxy,xm->tlmy", departure, x_table, precision=high)
    partial_modes = jnp.einsum("tlmy,yn->tlmn", half_proj, y_table, precision=high)
    partial_modes = partial_modes.reshape(tracers, levels, MX * MY)
    coeffs = lax.psum(partial_modes, ("gx", "gy"))
    modal = coeffs.reshape(tracers, levels, MX, MY)
    large_scale = jnp.einsum("tlmn,yn->tlmy", modal, y_table, precision=high)
    large_scale = jnp.einsum("tlmy,xm->tlxy", large_scale, x_table, precision=high)
    nudged = field + 0.5 * large_scale
    xpos = x_first + jnp.arange(strip_cols, dtype=jnp.int32)
    ypos = y_first + jnp.arange(band_rows, dtype=jnp.int32)
    east_face = jnp.where(xpos[None, :, None] == nx_total - 1, jnp.float32(0.0), east_wind)
    north_face = jnp.where(ypos[None, None, :] == ny_total - 1, jnp.float32(0.0), north_wind)
    east_below = shifted(east_face[:, -1:, :], "gx", 1)
    north_below = shifted(north_face[:, :, -1:], "gy", 1)
    east_ext = jnp.concatenate([east_below, east_face, jnp.zeros_like(east_below)], axis=1)
    east_ext = jnp.pad(east_ext, ((0, 0), (0, 0), (1, 1)))
    north_ext = jnp.concatenate([north_below, north_face, jnp.zeros_like(north_below)], axis=2)
    north_ext = jnp.pad(north_ext, ((0, 0), (1, 1), (0, 0)))
    wind_ext = jnp.stack([east_ext, north_ext])
    advected = nudged
    for sweep in range(2):
        field_ext = padded(advected, (("gx", 2), ("gy", 3)), 1)
        advected = upwind(field_ext, wind_ext)
    return (advected, coeffs)


def solution(mesh):
    placed = (
        P(None, None, "gx", "gy"),
        P(None, None, "gx", "gy"),
        P(None, "gx", "gy"),
        P(None, "gx", "gy"),
    )
    return jax.shard_map(
        shards,
        mesh=mesh,
        in_specs=placed,
        out_specs=(P(None, None, "gx", "gy"), P()),
        check_vma=False,
    )
```

profile of v0, /device:TPU:8, one launch (start us, length us, event | category | flops | bytes accessed | tf_op | source)
XLA Modules:
  0.0 223.3 jit_solution(13646085363777777054)
XLA Ops:
  7.8 4.2 %fusion.12 = f32[64,6,16,128]{3,0,2,1:T(8,128)S(1)} fusion(f32[6,16,16,128]{3,2,1,0:T(8,128)} %param.5, f32[6,16,16,128]{3,2,1,0:T(8,128)} %param.4, f32[64]{0:T(128)S(1)} %compare_select_fusion, s32[16]{0:T(128)S(1)} %multiply_add_fusion.1), kind=kOutput, calls=%fused_computation.29 | convolution fusion | flops 151195648 | bytes 4718912 | tf_op jit(solution)/shard_map/tlxy,xm->tlmy/dot_general | solution.py:67
  12.0 2.7 %fusion = f32[6,16,64,64]{3,2,1,0:T(8,128)S(1)} fusion(f32[64,6,16,128]{3,0,2,1:T(8,128)S(1)} %fusion.12, f32[64]{0:T(128)S(1)} %compare_select_fusion, s32[128]{0:T(128)S(1)} %multiply_add_fusion), kind=kOutput, calls=%fused_computation | convolution fusion | flops 604012544 | bytes 4719360 | tf_op jit(solution)/shard_map/tlmy,yn->tlmn/dot_general | solution.py:68
  14.7 1.9 reshape.47
  16.8 3.4 %collective-permute-start.5 = (f32[16,16,1]{2,1,0:T(8,128)S(1)}, f32[16,16,1]{2,1,0:T(8,128)S(1)}, u32[]{:S(2)}, u32[]{:S(2)}) collective-permute-start(f32[16,16,1]{2,1,0:T(8,128)S(1)} %slice.119), channel_id=1, source_target_pairs={{0,1},{2,3},{4,5},{6,7},{8,9},{10,11},{12,13},{14,15},{16,17},{18,... | collective-permute-start | bytes 3080 | tf_op jit(solution)/shard_map/ppermute | solution.py:14
  20.3 2.1 collective-permute-start
  24.1 125.8 %all-reduce.4.cloned.1.call-done = f32[6,16,4096]{2,1,0:T(8,128)} async-done(((f32[6,16,4096]{2,1,0:T(8,128)}), f32[6,16,4096]{2,1,0:T(8,128)}) %all-reduce.4.cloned.1.call-update) | async-done | bytes 1572880 | tf_op jit(solution)/shard_map/psum | solution.py:70
  149.9 2.4 %reshape.48 = f32[6,16,64,64]{3,2,1,0:T(8,128)S(1)} reshape(f32[6,16,4096]{2,1,0:T(8,128)} %all-reduce.4.cloned.1.call-done) | data formatting | bytes 3145728 | tf_op jit(solution)/shard_map/reshape | solution.py:71
  152.3 3.6 %fusion.18 = f32[6,16,64,128]{3,2,1,0:T(8,128)S(1)} fusion(f32[6,16,64,64]{3,2,1,0:T(8,128)S(1)} %reshape.48, f32[64]{0:T(128)} %copy-done.17, s32[128]{0:T(128)} %copy-done.21), kind=kOutput, calls=%fused_computation.41 | convolution fusion | flops 604012544 | bytes 4719360 | tf_op jit(solution)/shard_map/tlmn,yn->tlmy/dot_general | solution.py:72
  156.0 1.7 fusion.7
  157.7 1.9 collective-permute-start.2
  159.7 2.4 %collective-permute-start.1 = (f32[6,16,1,128]{3,2,1,0:T(1,128)S(1)}, f32[6,16,1,128]{3,2,1,0:T(1,128)S(1)}, u32[]{:S(2)}, u32[]{:S(2)}) collective-permute-start(f32[6,16,1,128]{3,2,1,0:T(1,128)S(1)} %get-tuple-element.8), channel_id=1, source_target_pairs={{0,2},{2,4},{4,6},{6,8},{8,10},{10,12},{12,14},{14,16},{16,18},{18... | collective-permute-start | bytes 147464 | tf_op jit(solution)/shard_map/ppermute | solution.py:24
  162.9 3.1 %collective-permute-done.1 = f32[6,16,1,128]{3,2,1,0:T(1,128)S(1)} collective-permute-done((f32[6,16,1,128]{3,2,1,0:T(1,128)S(1)}, f32[6,16,1,128]{3,2,1,0:T(1,128)S(1)}, u32[]{:S(2)}, u32[]{:S(2)}) %collective-permute-start.1) | collective-permute-done | bytes 49184 | tf_op jit(solution)/shard_map/ppermute | solution.py:24
  166.6 1.3 copy.6
  167.9 3.3 %collective-permute-start.3 = (f32[6,16,18,1]{2,1,3,0:T(8,128)}, f32[6,16,18,1]{2,1,3,0:T(8,128)S(1)}, u32[]{:S(2)}, u32[]{:S(2)}) collective-permute-start(f32[6,16,18,1]{2,1,3,0:T(8,128)} %copy.6), channel_id=1, source_target_pairs={{0,1},{2,3},{4,5},{6,7},{8,9},{10,11},{12,13},{14,15},{16,17},{18,... | collective-permute-start | bytes 20744 | tf_op jit(solution)/shard_map/ppermute | solution.py:24
  171.9 1.3 collective-permute-start.4
  173.1 2.2 fusion.15
  176.0 1.9 collective-permute-done.4
  177.9 1.5 copy.9
  179.4 2.3 %pad_maximum_fusion = f32[6,16,18,130]{3,2,1,0:T(8,128)S(1)} fusion(f32[6,16,18,1]{3,2,1,0:T(8,128)S(1)} %copy.9, f32[6,16,1,128]{3,2,1,0:T(1,128)} %copy-done.11, f32[6,16,16,128]{3,2,1,0:T(8,128)S(1)} %fusion.7, f32[6,16,1,128]{3,2,1,0:T(1,128)} %copy-done.13, f32[6,16,18,1]{3,2,1,0:T(8,128)S(1)} %copy.8), kind=kLoop, calls=%fused_computation.8 | loop fusion | flops 898560 | bytes 1797120 | tf_op jit(solution)/shard_map/concatenate | solution.py:26
  182.8 1.3 fusion.4
  184.8 1.9 collective-permute-start.7
  186.7 2.6 %collective-permute-start.6 = (f32[6,16,1,128]{3,2,1,0:T(1,128)S(1)}, f32[6,16,1,128]{3,2,1,0:T(1,128)S(1)}, u32[]{:S(2)}, u32[]{:S(2)}) collective-permute-start(f32[6,16,1,128]{3,2,1,0:T(1,128)S(1)} %get-tuple-element.6), channel_id=1, source_target_pairs={{0,2},{2,4},{4,6},{6,8},{8,10},{10,12},{12,14},{14,16},{16,18},{18... | collective-permute-start | bytes 147464 | tf_op jit(solution)/shard_map/ppermute | solution.py:24
  189.3 3.9 %collective-permute-done.6 = f32[6,16,1,128]{3,2,1,0:T(1,128)S(1)} collective-permute-done((f32[6,16,1,128]{3,2,1,0:T(1,128)S(1)}, f32[6,16,1,128]{3,2,1,0:T(1,128)S(1)}, u32[]{:S(2)}, u32[]{:S(2)}) %collective-permute-start.6) | collective-permute-done | bytes 49184 | tf_op jit(solution)/shard_map/ppermute | solution.py:24
  193.4 1.4 fusion.41
  194.8 1.9 copy.12
  196.7 3.2 %collective-permute-start.8 = (f32[6,16,18,1]{2,1,3,0:T(8,128)S(1)}, f32[6,16,18,1]{2,1,3,0:T(8,128)S(1)}, u32[]{:S(2)}, u32[]{:S(2)}) collective-permute-start(f32[6,16,18,1]{2,1,3,0:T(8,128)S(1)} %copy.12), channel_id=1, source_target_pairs={{0,1},{2,3},{4,5},{6,7},{8,9},{10,11},{12,13},{14,15},{16,17},{18,... | collective-permute-start | bytes 20744 | tf_op jit(solution)/shard_map/ppermute | solution.py:24
  200.7 1.3 collective-permute-start.9
  202.7 4.0 %collective-permute-done.9 = f32[6,16,18,1]{2,1,3,0:T(8,128)S(1)} collective-permute-done((f32[6,16,18,1]{2,1,3,0:T(8,128)S(1)}, f32[6,16,18,1]{2,1,3,0:T(8,128)S(1)}, u32[]{:S(2)}, u32[]{:S(2)}) %collective-permute-start.9) | collective-permute-done | bytes 6944 | tf_op jit(solution)/shard_map/ppermute | solution.py:25
  206.6 1.7 copy.15
  208.3 2.7 %pad_maximum_fusion.1 = f32[6,16,18,130]{3,2,1,0:T(8,128)S(1)} fusion(f32[6,16,18,1]{3,2,1,0:T(8,128)} %copy.15, f32[6,16,1,128]{3,2,1,0:T(1,128)S(1)} %collective-permute-done.7, f32[6,16,16,128]{3,2,1,0:T(8,128)S(1)} %fusion.10, f32[6,16,1,128]{3,2,1,0:T(1,128)S(1)} %collective-permute-done.6, f32[6,16,18,1]{3,2,1,0:T(8,128)S(1)} %copy.14), kind=kLoop, calls=%fused_computation.12 | loop fusion | flops 898560 | bytes 1797120 | tf_op jit(solution)/shard_map/concatenate | solution.py:26
  212.4 1.3 fusion.5
  213.7 1.6 fusion.8
  (81 shorter events, 11.1 us)
Async XLA Ops:
  7.2 142.7 %all-reduce.4.cloned.1.call-start = ((), (), s32[]{:S(2)}) async-start(), calls=%async_computation | async-start | bytes 3145728 | tf_op jit(solution)/shard_map/psum | solution.py:70
  7.2 4.7 %copy-start.17 = (f32[64]{0:T(128)}, f32[64]{0:T(128)S(1)}, u32[]{:S(2)}) copy-start(f32[64]{0:T(128)S(1)} %compare_select_fusion) | copy-start | bytes 772
  7.8 4.2 %copy-start.21 = (s32[128]{0:T(128)}, s32[128]{0:T(128)S(1)}, u32[]{:S(2)}) copy-start(s32[128]{0:T(128)S(1)} %multiply_add_fusion) | copy-start | bytes 1540
  14.7 2.0 copy-start.15
  14.7 5.5 %copy-start.16 = (f32[16,16,128]{2,1,0:T(8,128)S(1)}, f32[16,16,128]{2,1,0:T(8,128)}, u32[]{:S(2)}) copy-start(f32[16,16,128]{2,1,0:T(8,128)} %param.6) | copy-start | bytes 393220
  16.8 6.4 %collective-permute-start.5 = (f32[16,16,1]{2,1,0:T(8,128)S(1)}, f32[16,16,1]{2,1,0:T(8,128)S(1)}, u32[]{:S(2)}, u32[]{:S(2)}) collective-permute-start(f32[16,16,1]{2,1,0:T(8,128)S(1)} %slice.119), channel_id=1, source_target_pairs={{0,1},{2,3},{4,5},{6,7},{8,9},{10,11},{12,13},{14,15},{16,17},{18,... | collective-permute-start | bytes 3080 | tf_op jit(solution)/shard_map/ppermute | solution.py:14
  20.3 2.9 %copy-start.9 = (f32[16,16,128]{2,1,0:T(8,128)}, f32[16,16,128]{2,1,0:T(8,128)S(1)}, u32[]{:S(2)}) copy-start(f32[16,16,128]{2,1,0:T(8,128)S(1)} %broadcast_select_fusion.1) | copy-start | bytes 393220
  20.3 141.7 %collective-permute-start = (f32[16,1,128]{2,1,0:T(1,128)S(1)}, f32[16,1,128]{2,1,0:T(1,128)S(1)}, u32[]{:S(2)}, u32[]{:S(2)}) collective-permute-start(f32[16,1,128]{2,1,0:T(1,128)S(1)} %slice.110), channel_id=1, source_target_pairs={{0,2},{2,4},{4,6},{6,8},{8,10},{10,12},{12,14},{14,16},{16,18},{18... | collective-permute-start | bytes 24584 | tf_op jit(solution)/shard_map/ppermute | solution.py:14
  152.3 3.6 %copy-start.8 = (f32[6,16,16,128]{3,2,1,0:T(8,128)S(1)}, f32[6,16,16,128]{3,2,1,0:T(8,128)}, u32[]{:S(2)}) copy-start(f32[6,16,16,128]{3,2,1,0:T(8,128)} %param.4) | copy-start | bytes 2359300
  152.3 3.6 %copy-start.18 = (f32[64]{0:T(128)S(1)}, f32[64]{0:T(128)}, u32[]{:S(2)}) copy-start(f32[64]{0:T(128)} %copy-done.17) | copy-start | bytes 772
  152.3 3.6 %copy-start.20 = (s32[16]{0:T(128)S(1)}, s32[16]{0:T(128)}, u32[]{:S(2)}) copy-start(s32[16]{0:T(128)} %copy-done.19) | copy-start | bytes 196
  155.9 6.1 %copy-start.10 = (f32[16,16,128]{2,1,0:T(8,128)S(1)}, f32[16,16,128]{2,1,0:T(8,128)}, u32[]{:S(2)}) copy-start(f32[16,16,128]{2,1,0:T(8,128)} %copy-done.9) | copy-start | bytes 393220
  156.0 6.1 %copy-start.22 = (f32[18]{0:T(128)S(1)}, f32[18]{0:T(128)}, u32[]{:S(2)}) copy-start(f32[18]{0:T(128)} %pad.47.clone) | copy-start | bytes 220
  157.7 5.1 %collective-permute-start.2 = (f32[6,16,1,128]{3,2,1,0:T(1,128)S(1)}, f32[6,16,1,128]{3,2,1,0:T(1,128)S(1)}, u32[]{:S(2)}, u32[]{:S(2)}) collective-permute-start(f32[6,16,1,128]{3,2,1,0:T(1,128)S(1)} %get-tuple-element.9), channel_id=1, source_target_pairs={{2,0},{4,2},{6,4},{8,6},{10,8},{12,10},{14,12},{16,14},{18,16},{20... | collective-permute-start | bytes 147464 | tf_op jit(solution)/shard_map/ppermute | solution.py:25
  159.7 6.3 %collective-permute-start.1 = (f32[6,16,1,128]{3,2,1,0:T(1,128)S(1)}, f32[6,16,1,128]{3,2,1,0:T(1,128)S(1)}, u32[]{:S(2)}, u32[]{:S(2)}) collective-permute-start(f32[6,16,1,128]{3,2,1,0:T(1,128)S(1)} %get-tuple-element.8), channel_id=1, source_target_pairs={{0,2},{2,4},{4,6},{6,8},{8,10},{10,12},{12,14},{14,16},{16,18},{18... | collective-permute-start | bytes 147464 | tf_op jit(solution)/shard_map/ppermute | solution.py:24
  162.9 3.7 %copy-start.11 = (f32[6,16,1,128]{3,2,1,0:T(1,128)}, f32[6,16,1,128]{3,2,1,0:T(1,128)S(1)}, u32[]{:S(2)}) copy-start(f32[6,16,1,128]{3,2,1,0:T(1,128)S(1)} %collective-permute-done.2) | copy-start | bytes 147460
  167.9 7.5 %collective-permute-start.3 = (f32[6,16,18,1]{2,1,3,0:T(8,128)}, f32[6,16,18,1]{2,1,3,0:T(8,128)S(1)}, u32[]{:S(2)}, u32[]{:S(2)}) collective-permute-start(f32[6,16,18,1]{2,1,3,0:T(8,128)} %copy.6), channel_id=1, source_target_pairs={{0,1},{2,3},{4,5},{6,7},{8,9},{10,11},{12,13},{14,15},{16,17},{18,... | collective-permute-start | bytes 20744 | tf_op jit(solution)/shard_map/ppermute | solution.py:24
  171.9 6.1 %collective-permute-start.4 = (f32[6,16,18,1]{2,1,3,0:T(8,128)S(1)}, f32[6,16,18,1]{2,1,3,0:T(8,128)}, u32[]{:S(2)}, u32[]{:S(2)}) collective-permute-start(f32[6,16,18,1]{2,1,3,0:T(8,128)S(1)} %copy.7), channel_id=1, source_target_pairs={{1,0},{3,2},{5,4},{7,6},{9,8},{11,10},{13,12},{15,14},{17,16},{19,... | collective-permute-start | bytes 20744 | tf_op jit(solution)/shard_map/ppermute | solution.py:25
  179.4 2.3 %copy-start.4 = (f32[16,17,130]{2,1,0:T(8,128)S(1)}, f32[16,17,130]{2,1,0:T(8,128)}, u32[]{:S(2)}) copy-start(f32[16,17,130]{2,1,0:T(8,128)} %get-tuple-element.12) | copy-start | bytes 424324
  179.4 2.3 %copy-start.6 = (f32[16,17,130]{2,1,0:T(8,128)S(1)}, f32[16,17,130]{2,1,0:T(8,128)}, u32[]{:S(2)}) copy-start(f32[16,17,130]{2,1,0:T(8,128)} %get-tuple-element.13) | copy-start | bytes 424324
  181.8 1.0 copy-start.2
  181.8 1.0 copy-start.12
  181.8 1.0 copy-start.14
  184.8 4.6 %collective-permute-start.7 = (f32[6,16,1,128]{3,2,1,0:T(1,128)S(1)}, f32[6,16,1,128]{3,2,1,0:T(1,128)S(1)}, u32[]{:S(2)}, u32[]{:S(2)}) collective-permute-start(f32[6,16,1,128]{3,2,1,0:T(1,128)S(1)} %get-tuple-element.7), channel_id=1, source_target_pairs={{2,0},{4,2},{6,4},{8,6},{10,8},{12,10},{14,12},{16,14},{18,16},{20... | collective-permute-start | bytes 147464 | tf_op jit(solution)/shard_map/ppermute | solution.py:25
  186.7 6.5 %collective-permute-start.6 = (f32[6,16,1,128]{3,2,1,0:T(1,128)S(1)}, f32[6,16,1,128]{3,2,1,0:T(1,128)S(1)}, u32[]{:S(2)}, u32[]{:S(2)}) collective-permute-start(f32[6,16,1,128]{3,2,1,0:T(1,128)S(1)} %get-tuple-element.6), channel_id=1, source_target_pairs={{0,2},{2,4},{4,6},{6,8},{8,10},{10,12},{12,14},{14,16},{16,18},{18... | collective-permute-start | bytes 147464 | tf_op jit(solution)/shard_map/ppermute | solution.py:24
  196.7 5.2 %collective-permute-start.8 = (f32[6,16,18,1]{2,1,3,0:T(8,128)S(1)}, f32[6,16,18,1]{2,1,3,0:T(8,128)S(1)}, u32[]{:S(2)}, u32[]{:S(2)}) collective-permute-start(f32[6,16,18,1]{2,1,3,0:T(8,128)S(1)} %copy.12), channel_id=1, source_target_pairs={{0,1},{2,3},{4,5},{6,7},{8,9},{10,11},{12,13},{14,15},{16,17},{18,... | collective-permute-start | bytes 20744 | tf_op jit(solution)/shard_map/ppermute | solution.py:24
  200.7 6.0 %collective-permute-start.9 = (f32[6,16,18,1]{2,1,3,0:T(8,128)S(1)}, f32[6,16,18,1]{2,1,3,0:T(8,128)S(1)}, u32[]{:S(2)}, u32[]{:S(2)}) collective-permute-start(f32[6,16,18,1]{2,1,3,0:T(8,128)S(1)} %copy.13), channel_id=1, source_target_pairs={{1,0},{3,2},{5,4},{7,6},{9,8},{11,10},{13,12},{15,14},{17,16},{19,... | collective-permute-start | bytes 20744 | tf_op jit(solution)/shard_map/ppermute | solution.py:25
  208.3 2.7 %copy-start.5 = (f32[16,17,130]{2,1,0:T(8,128)S(1)}, f32[16,17,130]{2,1,0:T(8,128)}, u32[]{:S(2)}) copy-start(f32[16,17,130]{2,1,0:T(8,128)} %get-tuple-element.12) | copy-start | bytes 424324
  208.3 2.8 %copy-start.7 = (f32[16,17,130]{2,1,0:T(8,128)S(1)}, f32[16,17,130]{2,1,0:T(8,128)}, u32[]{:S(2)}) copy-start(f32[16,17,130]{2,1,0:T(8,128)} %get-tuple-element.13) | copy-start | bytes 424324
  211.1 1.3 copy-start
  211.1 1.3 copy-start.3
  213.7 1.6 copy-start.1
  (2 other events, 1.1 us)
Sparse Core Ops, SparseCore 0:
  16.8 133.0 all-reduce.3
where the time goes:
time: 224 us; the launch traced here: 223 us
  waiting for transfers between devices  139 us (62%)
  starting transfers between devices  23.5 us (10%)
  local copies, waits for them, and re-layouts  19.4 us (9%)
  other arithmetic  15 us (7%)
  between operations  14.6 us (7%)
  matrix products  12.1 us (5%)
    psum x1, waiting for transfers between devices, shards(): coeffs = lax.psum(partial_modes, ('gx', 'gy'))  126 us
    ppermute x4, starting transfers between devices, padded(): before = lax.ppermute(last, axis, up)  11.6 us
    ppermute x4, waiting for transfers between devices, padded(): before = lax.ppermute(last, axis, up)  6.99 us
    ppermute x4, starting transfers between devices, padded(): after = lax.ppermute(first, axis, down)  6.4 us
    ppermute x4, waiting for transfers between devices, padded(): after = lax.ppermute(first, axis, down)  5.89 us
    ppermute x2, starting transfers between devices, shifted(): lax.ppermute(value, axis, [(source, source + steps) for source in range(f...  5.5 us
    concatenate x4, other arithmetic, padded(): x = jnp.concatenate([before, x, after], axis=dim)  5.4 us
  transfers between devices with their start and end apart: 11, of which 5 were waited for; matrix products, arithmetic and copies ran while one was open for 7% of the time, Pallas kernels for 0%

commit v1 on v0

--- a/solution.py
+++ b/solution.py
@@ -67,7 +67,7 @@
     half_proj = jnp.einsum("tlxy,xm->tlmy", departure, x_table, precision=high)
     partial_modes = jnp.einsum("tlmy,yn->tlmn", half_proj, y_table, precision=high)
     partial_modes = partial_modes.reshape(tracers, levels, MX * MY)
-    coeffs = lax.psum(partial_modes, ("gx", "gy"))
+    coeffs = lax.psum(lax.psum(partial_modes, "gy"), "gx")
     modal = coeffs.reshape(tracers, levels, MX, MY)
     large_scale = jnp.einsum("tlmn,yn->tlmy", modal, y_table, precision=high)
     large_scale = jnp.einsum("tlmy,xm->tlxy", large_scale, x_table, precision=high)

time: 224 us -> 243 us (1.085)
  waiting for transfers between devices: 139 us -> 158 us
    psum x1 -> x2, waiting for transfers between devices: 126 us -> 145 us  [shards(): coeffs = lax.psum(lax.psum(partial_modes, 'gy'), 'gx')]
  transfers between devices with their start and end apart: 11 -> 12, of which waited for: 5 -> 6; matrix products, arithmetic and copies ran while one was open for 7% -> 6% of each run, Pallas kernels for 0% -> 0%
where the time goes in v1:
time: 243 us; the launch traced here: 242 us
  waiting for transfers between devices  158 us (65%)
  starting transfers between devices  22.7 us (9%)
  local copies, waits for them, and re-layouts  19.3 us (8%)
  other arithmetic  15 us (6%)
  between operations  14.6 us (6%)
  matrix products  12.2 us (5%)
    psum x2, waiting for transfers between devices, shards(): coeffs = lax.psum(lax.psum(partial_modes, 'gy'), 'gx')  145 us
    ppermute x4, starting transfers between devices, padded(): before = lax.ppermute(last, axis, up)  11.6 us
    ppermute x4, waiting for transfers between devices, padded(): before = lax.ppermute(last, axis, up)  6.99 us
    ppermute x4, starting transfers between devices, padded(): after = lax.ppermute(first, axis, down)  6.4 us
    ppermute x4, waiting for transfers between devices, padded(): after = lax.ppermute(first, axis, down)  5.89 us
    concatenate x4, other arithmetic, padded(): x = jnp.concatenate([before, x, after], axis=dim)  5.4 us
  transfers between devices with their start and end apart: 12, of which 6 were waited for; matrix products, arithmetic and copies ran while one was open for 6% of the time, Pallas kernels for 0%

profile of v1, /device:TPU:8, one launch (start us, length us, event | category | flops | bytes accessed | tf_op | source)
XLA Modules:
  0.0 242.1 jit_solution(16600559874720118165)
XLA Ops:
  7.8 4.2 %fusion.12 = f32[64,6,16,128]{3,0,2,1:T(8,128)S(1)} fusion(f32[6,16,16,128]{3,2,1,0:T(8,128)} %param.5, f32[6,16,16,128]{3,2,1,0:T(8,128)} %param.4, f32[64]{0:T(128)S(1)} %compare_select_fusion, s32[16]{0:T(128)S(1)} %multiply_add_fusion.1), kind=kOutput, calls=%fused_computation.29 | convolution fusion | flops 151195648 | bytes 4718912 | tf_op jit(solution)/shard_map/tlxy,xm->tlmy/dot_general | solution.py:67
  12.0 2.7 %fusion = f32[6,16,64,64]{3,2,1,0:T(8,128)S(1)} fusion(f32[64,6,16,128]{3,0,2,1:T(8,128)S(1)} %fusion.12, f32[64]{0:T(128)S(1)} %compare_select_fusion, s32[128]{0:T(128)S(1)} %multiply_add_fusion), kind=kOutput, calls=%fused_computation | convolution fusion | flops 604012544 | bytes 4719360 | tf_op jit(solution)/shard_map/tlmy,yn->tlmn/dot_general | solution.py:68
  14.7 1.9 reshape.47
  16.7 52.7 %all-reduce.5.cloned.1.call-done = f32[6,16,4096]{2,1,0:T(8,128)} async-done(((f32[6,16,4096]{2,1,0:T(8,128)}), f32[6,16,4096]{2,1,0:T(8,128)}) %all-reduce.5.cloned.1.call-update) | async-done | bytes 1572880 | tf_op jit(solution)/shard_map/psum | solution.py:70
  69.6 2.5 %collective-permute-start.5 = (f32[16,16,1]{2,1,0:T(8,128)S(1)}, f32[16,16,1]{2,1,0:T(8,128)S(1)}, u32[]{:S(2)}, u32[]{:S(2)}) collective-permute-start(f32[16,16,1]{2,1,0:T(8,128)S(1)} %slice.119), channel_id=1, source_target_pairs={{0,1},{2,3},{4,5},{6,7},{8,9},{10,11},{12,13},{14,15},{16,17},{18,... | collective-permute-start | bytes 3080 | tf_op jit(solution)/shard_map/ppermute | solution.py:14
  72.2 2.1 collective-permute-start
  75.9 92.6 %all-reduce.7.cloned.1.call-done = f32[6,16,4096]{2,1,0:T(8,128)} async-done(((f32[6,16,4096]{2,1,0:T(8,128)}), f32[6,16,4096]{2,1,0:T(8,128)}) %all-reduce.7.cloned.1.call-update) | async-done | bytes 1572880 | tf_op jit(solution)/shard_map/psum | solution.py:70
  168.6 2.4 reshape.48
  171.0 3.6 %fusion.18 = f32[6,16,64,128]{3,2,1,0:T(8,128)S(1)} fusion(f32[6,16,64,64]{3,2,1,0:T(8,128)S(1)} %reshape.48, f32[64]{0:T(128)} %copy-done.17, s32[128]{0:T(128)} %copy-done.21), kind=kOutput, calls=%fused_computation.41 | convolution fusion | flops 604012544 | bytes 4719360 | tf_op jit(solution)/shard_map/tlmn,yn->tlmy/dot_general | solution.py:72
  174.7 1.7 fusion.7
  176.5 1.9 collective-permute-start.2
  178.4 2.4 collective-permute-start.1
  181.6 3.1 %collective-permute-done.1 = f32[6,16,1,128]{3,2,1,0:T(1,128)S(1)} collective-permute-done((f32[6,16,1,128]{3,2,1,0:T(1,128)S(1)}, f32[6,16,1,128]{3,2,1,0:T(1,128)S(1)}, u32[]{:S(2)}, u32[]{:S(2)}) %collective-permute-start.1) | collective-permute-done | bytes 49184 | tf_op jit(solution)/shard_map/ppermute | solution.py:24
  185.4 1.3 copy.6
  186.6 3.4 %collective-permute-start.3 = (f32[6,16,18,1]{2,1,3,0:T(8,128)}, f32[6,16,18,1]{2,1,3,0:T(8,128)S(1)}, u32[]{:S(2)}, u32[]{:S(2)}) collective-permute-start(f32[6,16,18,1]{2,1,3,0:T(8,128)} %copy.6), channel_id=1, source_target_pairs={{0,1},{2,3},{4,5},{6,7},{8,9},{10,11},{12,13},{14,15},{16,17},{18,... | collective-permute-start | bytes 20744 | tf_op jit(solution)/shard_map/ppermute | solution.py:24
  190.7 1.3 collective-permute-start.4
  192.0 2.2 fusion.15
  194.8 1.9 collective-permute-done.4
  196.8 1.5 copy.9
  198.3 2.3 pad_maximum_fusion
  201.6 1.3 fusion.4
  203.6 1.9 collective-permute-start.7
  205.5 2.6 %collective-permute-start.6 = (f32[6,16,1,128]{3,2,1,0:T(1,128)S(1)}, f32[6,16,1,128]{3,2,1,0:T(1,128)S(1)}, u32[]{:S(2)}, u32[]{:S(2)}) collective-permute-start(f32[6,16,1,128]{3,2,1,0:T(1,128)S(1)} %get-tuple-element.6), channel_id=1, source_target_pairs={{0,2},{2,4},{4,6},{6,8},{8,10},{10,12},{12,14},{14,16},{16,18},{18... | collective-permute-start | bytes 147464 | tf_op jit(solution)/shard_map/ppermute | solution.py:24
  208.2 3.9 %collective-permute-done.6 = f32[6,16,1,128]{3,2,1,0:T(1,128)S(1)} collective-permute-done((f32[6,16,1,128]{3,2,1,0:T(1,128)S(1)}, f32[6,16,1,128]{3,2,1,0:T(1,128)S(1)}, u32[]{:S(2)}, u32[]{:S(2)}) %collective-permute-start.6) | collective-permute-done | bytes 49184 | tf_op jit(solution)/shard_map/ppermute | solution.py:24
  212.2 1.4 fusion.41
  213.6 1.9 copy.12
  215.6 3.2 %collective-permute-start.8 = (f32[6,16,18,1]{2,1,3,0:T(8,128)S(1)}, f32[6,16,18,1]{2,1,3,0:T(8,128)S(1)}, u32[]{:S(2)}, u32[]{:S(2)}) collective-permute-start(f32[6,16,18,1]{2,1,3,0:T(8,128)S(1)} %copy.12), channel_id=1, source_target_pairs={{0,1},{2,3},{4,5},{6,7},{8,9},{10,11},{12,13},{14,15},{16,17},{18,... | collective-permute-start | bytes 20744 | tf_op jit(solution)/shard_map/ppermute | solution.py:24
  219.5 1.3 collective-permute-start.9
  221.5 4.0 %collective-permute-done.9 = f32[6,16,18,1]{2,1,3,0:T(8,128)S(1)} collective-permute-done((f32[6,16,18,1]{2,1,3,0:T(8,128)S(1)}, f32[6,16,18,1]{2,1,3,0:T(8,128)S(1)}, u32[]{:S(2)}, u32[]{:S(2)}) %collective-permute-start.9) | collective-permute-done | bytes 6944 | tf_op jit(solution)/shard_map/ppermute | solution.py:25
  225.4 1.7 copy.15
  227.1 2.7 %pad_maximum_fusion.1 = f32[6,16,18,130]{3,2,1,0:T(8,128)S(1)} fusion(f32[6,16,18,1]{3,2,1,0:T(8,128)} %copy.15, f32[6,16,1,128]{3,2,1,0:T(1,128)S(1)} %collective-permute-done.7, f32[6,16,16,128]{3,2,1,0:T(8,128)S(1)} %fusion.10, f32[6,16,1,128]{3,2,1,0:T(1,128)S(1)} %collective-permute-done.6, f32[6,16,18,1]{3,2,1,0:T(8,128)S(1)} %copy.14), kind=kLoop, calls=%fused_computation.12 | loop fusion | flops 898560 | bytes 1797120 | tf_op jit(solution)/shard_map/concatenate | solution.py:26
  232.5 1.6 fusion.8
  (84 shorter events, 12.3 us)
Async XLA Ops:
  7.2 62.3 %all-reduce.5.cloned.1.call-start = ((), (), s32[]{:S(2)}) async-start(), calls=%async_computation | async-start | bytes 3145728 | tf_op jit(solution)/shard_map/psum | solution.py:70
  7.2 4.7 %copy-start.17 = (f32[64]{0:T(128)}, f32[64]{0:T(128)S(1)}, u32[]{:S(2)}) copy-start(f32[64]{0:T(128)S(1)} %compare_select_fusion) | copy-start | bytes 772
  7.8 4.2 %copy-start.21 = (s32[128]{0:T(128)}, s32[128]{0:T(128)S(1)}, u32[]{:S(2)}) copy-start(s32[128]{0:T(128)S(1)} %multiply_add_fusion) | copy-start | bytes 1540
  16.6 52.9 %copy-start.15 = (f32[16,16,128]{2,1,0:T(8,128)S(1)}, f32[16,16,128]{2,1,0:T(8,128)}, u32[]{:S(2)}) copy-start(f32[16,16,128]{2,1,0:T(8,128)} %param.7) | copy-start | bytes 393220
  16.6 55.5 %copy-start.16 = (f32[16,16,128]{2,1,0:T(8,128)S(1)}, f32[16,16,128]{2,1,0:T(8,128)}, u32[]{:S(2)}) copy-start(f32[16,16,128]{2,1,0:T(8,128)} %param.6) | copy-start | bytes 393220
  16.6 151.9 %all-reduce.7.cloned.1.call-start = ((), (), s32[]{:S(2)}) async-start(), calls=%async_computation.1 | async-start | bytes 3145728 | tf_op jit(solution)/shard_map/psum | solution.py:70
  69.6 5.4 %collective-permute-start.5 = (f32[16,16,1]{2,1,0:T(8,128)S(1)}, f32[16,16,1]{2,1,0:T(8,128)S(1)}, u32[]{:S(2)}, u32[]{:S(2)}) collective-permute-start(f32[16,16,1]{2,1,0:T(8,128)S(1)} %slice.119), channel_id=1, source_target_pairs={{0,1},{2,3},{4,5},{6,7},{8,9},{10,11},{12,13},{14,15},{16,17},{18,... | collective-permute-start | bytes 3080 | tf_op jit(solution)/shard_map/ppermute | solution.py:14
  72.2 2.8 %copy-start.9 = (f32[16,16,128]{2,1,0:T(8,128)}, f32[16,16,128]{2,1,0:T(8,128)S(1)}, u32[]{:S(2)}) copy-start(f32[16,16,128]{2,1,0:T(8,128)S(1)} %broadcast_select_fusion.1) | copy-start | bytes 393220
  72.2 108.6 %collective-permute-start = (f32[16,1,128]{2,1,0:T(1,128)S(1)}, f32[16,1,128]{2,1,0:T(1,128)S(1)}, u32[]{:S(2)}, u32[]{:S(2)}) collective-permute-start(f32[16,1,128]{2,1,0:T(1,128)S(1)} %slice.110), channel_id=1, source_target_pairs={{0,2},{2,4},{4,6},{6,8},{8,10},{10,12},{12,14},{14,16},{16,18},{18... | collective-permute-start | bytes 24584 | tf_op jit(solution)/shard_map/ppermute | solution.py:14
  171.0 3.7 %copy-start.8 = (f32[6,16,16,128]{3,2,1,0:T(8,128)S(1)}, f32[6,16,16,128]{3,2,1,0:T(8,128)}, u32[]{:S(2)}) copy-start(f32[6,16,16,128]{3,2,1,0:T(8,128)} %param.4) | copy-start | bytes 2359300
  171.0 3.7 %copy-start.18 = (f32[64]{0:T(128)S(1)}, f32[64]{0:T(128)}, u32[]{:S(2)}) copy-start(f32[64]{0:T(128)} %copy-done.17) | copy-start | bytes 772
  171.0 3.7 %copy-start.20 = (s32[16]{0:T(128)S(1)}, s32[16]{0:T(128)}, u32[]{:S(2)}) copy-start(s32[16]{0:T(128)} %copy-done.19) | copy-start | bytes 196
  174.7 6.1 %copy-start.10 = (f32[16,16,128]{2,1,0:T(8,128)S(1)}, f32[16,16,128]{2,1,0:T(8,128)}, u32[]{:S(2)}) copy-start(f32[16,16,128]{2,1,0:T(8,128)} %copy-done.9) | copy-start | bytes 393220
  174.7 6.1 %copy-start.22 = (f32[18]{0:T(128)S(1)}, f32[18]{0:T(128)}, u32[]{:S(2)}) copy-start(f32[18]{0:T(128)} %pad.47.clone) | copy-start | bytes 220
  176.5 5.1 %collective-permute-start.2 = (f32[6,16,1,128]{3,2,1,0:T(1,128)S(1)}, f32[6,16,1,128]{3,2,1,0:T(1,128)S(1)}, u32[]{:S(2)}, u32[]{:S(2)}) collective-permute-start(f32[6,16,1,128]{3,2,1,0:T(1,128)S(1)} %get-tuple-element.9), channel_id=1, source_target_pairs={{2,0},{4,2},{6,4},{8,6},{10,8},{12,10},{14,12},{16,14},{18,16},{20... | collective-permute-start | bytes 147464 | tf_op jit(solution)/shard_map/ppermute | solution.py:25
  178.4 6.3 %collective-permute-start.1 = (f32[6,16,1,128]{3,2,1,0:T(1,128)S(1)}, f32[6,16,1,128]{3,2,1,0:T(1,128)S(1)}, u32[]{:S(2)}, u32[]{:S(2)}) collective-permute-start(f32[6,16,1,128]{3,2,1,0:T(1,128)S(1)} %get-tuple-element.8), channel_id=1, source_target_pairs={{0,2},{2,4},{4,6},{6,8},{8,10},{10,12},{12,14},{14,16},{16,18},{18... | collective-permute-start | bytes 147464 | tf_op jit(solution)/shard_map/ppermute | solution.py:24
  181.6 3.7 %copy-start.11 = (f32[6,16,1,128]{3,2,1,0:T(1,128)}, f32[6,16,1,128]{3,2,1,0:T(1,128)S(1)}, u32[]{:S(2)}) copy-start(f32[6,16,1,128]{3,2,1,0:T(1,128)S(1)} %collective-permute-done.2) | copy-start | bytes 147460
  186.6 7.5 %collective-permute-start.3 = (f32[6,16,18,1]{2,1,3,0:T(8,128)}, f32[6,16,18,1]{2,1,3,0:T(8,128)S(1)}, u32[]{:S(2)}, u32[]{:S(2)}) collective-permute-start(f32[6,16,18,1]{2,1,3,0:T(8,128)} %copy.6), channel_id=1, source_target_pairs={{0,1},{2,3},{4,5},{6,7},{8,9},{10,11},{12,13},{14,15},{16,17},{18,... | collective-permute-start | bytes 20744 | tf_op jit(solution)/shard_map/ppermute | solution.py:24
  190.7 6.1 %collective-permute-start.4 = (f32[6,16,18,1]{2,1,3,0:T(8,128)S(1)}, f32[6,16,18,1]{2,1,3,0:T(8,128)}, u32[]{:S(2)}, u32[]{:S(2)}) collective-permute-start(f32[6,16,18,1]{2,1,3,0:T(8,128)S(1)} %copy.7), channel_id=1, source_target_pairs={{1,0},{3,2},{5,4},{7,6},{9,8},{11,10},{13,12},{15,14},{17,16},{19,... | collective-permute-start | bytes 20744 | tf_op jit(solution)/shard_map/ppermute | solution.py:25
  198.2 2.3 copy-start.4
  198.3 2.3 copy-start.6
  200.6 1.0 copy-start.2
  200.6 1.0 copy-start.12
  203.6 4.6 %collective-permute-start.7 = (f32[6,16,1,128]{3,2,1,0:T(1,128)S(1)}, f32[6,16,1,128]{3,2,1,0:T(1,128)S(1)}, u32[]{:S(2)}, u32[]{:S(2)}) collective-permute-start(f32[6,16,1,128]{3,2,1,0:T(1,128)S(1)} %get-tuple-element.7), channel_id=1, source_target_pairs={{2,0},{4,2},{6,4},{8,6},{10,8},{12,10},{14,12},{16,14},{18,16},{20... | collective-permute-start | bytes 147464 | tf_op jit(solution)/shard_map/ppermute | solution.py:25
  205.5 6.5 %collective-permute-start.6 = (f32[6,16,1,128]{3,2,1,0:T(1,128)S(1)}, f32[6,16,1,128]{3,2,1,0:T(1,128)S(1)}, u32[]{:S(2)}, u32[]{:S(2)}) collective-permute-start(f32[6,16,1,128]{3,2,1,0:T(1,128)S(1)} %get-tuple-element.6), channel_id=1, source_target_pairs={{0,2},{2,4},{4,6},{6,8},{8,10},{10,12},{12,14},{14,16},{16,18},{18... | collective-permute-start | bytes 147464 | tf_op jit(solution)/shard_map/ppermute | solution.py:24
  215.6 5.2 %collective-permute-start.8 = (f32[6,16,18,1]{2,1,3,0:T(8,128)S(1)}, f32[6,16,18,1]{2,1,3,0:T(8,128)S(1)}, u32[]{:S(2)}, u32[]{:S(2)}) collective-permute-start(f32[6,16,18,1]{2,1,3,0:T(8,128)S(1)} %copy.12), channel_id=1, source_target_pairs={{0,1},{2,3},{4,5},{6,7},{8,9},{10,11},{12,13},{14,15},{16,17},{18,... | collective-permute-start | bytes 20744 | tf_op jit(solution)/shard_map/ppermute | solution.py:24
  219.5 6.0 %collective-permute-start.9 = (f32[6,16,18,1]{2,1,3,0:T(8,128)S(1)}, f32[6,16,18,1]{2,1,3,0:T(8,128)S(1)}, u32[]{:S(2)}, u32[]{:S(2)}) collective-permute-start(f32[6,16,18,1]{2,1,3,0:T(8,128)S(1)} %copy.13), channel_id=1, source_target_pairs={{1,0},{3,2},{5,4},{7,6},{9,8},{11,10},{13,12},{15,14},{17,16},{19,... | collective-permute-start | bytes 20744 | tf_op jit(solution)/shard_map/ppermute | solution.py:25
  227.1 2.7 %copy-start.5 = (f32[16,17,130]{2,1,0:T(8,128)S(1)}, f32[16,17,130]{2,1,0:T(8,128)}, u32[]{:S(2)}) copy-start(f32[16,17,130]{2,1,0:T(8,128)} %get-tuple-element.12) | copy-start | bytes 424324
  227.1 2.8 %copy-start.7 = (f32[16,17,130]{2,1,0:T(8,128)S(1)}, f32[16,17,130]{2,1,0:T(8,128)}, u32[]{:S(2)}) copy-start(f32[16,17,130]{2,1,0:T(8,128)} %get-tuple-element.13) | copy-start | bytes 424324
  229.9 1.3 copy-start
  229.9 1.3 copy-start.3
  232.5 1.6 copy-start.1
  (3 other events, 2.1 us)
Sparse Core Ops, SparseCore 0:
  16.8 52.6 all-reduce.4
  73.3 95.2 all-reduce.6
